TPU v7x, 32 devices: a whole 2x2x4 slice. The times are simulated.
32 devices in a mesh: rows: 4 (over z), chan: 8 (over y, x, core).
Axes of the slice: x: 2, y: 2, z: 4, core: 2. Of those that a mesh axis runs over, the one named last changes fastest.
Arguments:
- feats: bfloat16 [64, 1024, 1024], P('rows', 'chan'), may hold values from -140 to 140
- norm_gain: float32 [1024], P('chan'), may hold values from 0.1 to 1.9
- proj_weight: float32 [8, 1024], P(None, 'chan'), may hold values from -320 to 320
- chan_bias: float32 [1024], P('chan'), may hold values from -8 to -2
Outputs:
- mixed: bfloat16 [64, 1024, 1024], P('rows', 'chan')
All inputs are finite; a program needn't handle non-finite values.
Results may differ from a plain program's by a relative error of at most 0.001.
Values sent between devices are 32-bit elements; how exact they have to be, the bound alone decides.
A program may use at most 128 MiB of HBM per device.

v0:
```python
import jax
import jax.numpy as jnp
from jax import lax
from jax.sharding import PartitionSpec as P

CHANNELS = 1024
EPSILON = 1e-05


def advance(current, row_weights, row_rate):
    edge_zero = jnp.zeros_like(current[:, :1])
    left_side = jnp.concatenate([edge_zero, current[:, :-1]], axis=1)
    right_side = jnp.concatenate([current[:, 1:], edge_zero], axis=1)
    blended = (
        row_weights[0][None, :] * left_side
        + row_weights[1][None, :] * current
        + row_weights[2][None, :] * right_side
    )
    return (1.0 - row_rate) * blended


def coefficients(logits, chan_bias, offset):
    weights = jax.nn.softmax(logits[:, offset : offset + 3, :], axis=1)
    rates = jax.nn.sigmoid(logits[:, 6 + offset // 3, :][:, None, :] + chan_bias[None, :, None])
    return (weights, rates)


def sweep_rows(start, weights, rates, drive, reverse, keep):

    def sweep_row_step(current, inputs):
        row_weights, row_rate, row_drive = inputs
        current = advance(current, row_weights, row_rate) + row_drive
        return (current, current if keep else None)

    return lax.scan(sweep_row_step, start, (weights, rates, drive), reverse=reverse)


def carry_through(start, weights, rates, reverse):

    def carry_row_step(current, inputs):
        return (advance(current, inputs[0], inputs[1]), None)

    finished, _ = lax.scan(carry_row_step, start, (weights, rates), reverse=reverse)
    return finished


def shards(feats, norm_gain, proj_weight, chan_bias):
    logit_scale = CHANNELS ** (-0.5)
    values = feats.astype(jnp.float32)
    squares = jnp.sum(values * values, axis=1)
    square_total = lax.psum(squares, "chan")
    inverse = 1.0 / jnp.sqrt(square_total / CHANNELS + EPSILON)
    normed = values * inverse[:, None, :] * norm_gain[None, :, None]
    projected = jnp.einsum(
        "jc,rcw->rjw",
        proj_weight,
        normed,
        precision=lax.Precision.HIGHEST,
        preferred_element_type=jnp.float32,
    )
    logits = lax.psum(projected, "chan") * logit_scale
    down_weights, down_rate = coefficients(logits, chan_bias, 0)
    up_weights, up_rate = coefficients(logits, chan_bias, 3)
    down_drive = jnp.sqrt(down_rate) * normed
    up_drive = jnp.sqrt(up_rate) * normed
    anchor = jnp.zeros((feats.shape[1], feats.shape[2]), jnp.float32)
    down_local, _ = sweep_rows(anchor, down_weights, down_rate, down_drive, False, False)
    up_local, _ = sweep_rows(anchor, up_weights, up_rate, up_drive, True, False)
    gathered, down_ends, up_ends = (
        lax.all_gather(logits, "rows", axis=0, tiled=True),
        lax.all_gather(down_local, "rows", axis=0, tiled=True),
        lax.all_gather(up_local, "rows", axis=0, tiled=True),
    )
    position = lax.axis_index("rows")
    devices = lax.axis_size("rows")
    block_rows = logits.shape[0]
    local_chans = feats.shape[1]

    def down_visit(visited, current):
        visited = jnp.asarray(visited).astype(jnp.int32)
        block_logits = lax.dynamic_slice_in_dim(gathered, visited * block_rows, block_rows, 0)
        block_weights, block_rates = coefficients(block_logits, chan_bias, 0)
        block_end = lax.dynamic_slice_in_dim(down_ends, visited * local_chans, local_chans, 0)
        return carry_through(current, block_weights, block_rates, False) + block_end

    def up_visit(turn, current):
        visited = (devices - 1 - jnp.asarray(turn)).astype(jnp.int32)
        block_logits = lax.dynamic_slice_in_dim(gathered, visited * block_rows, block_rows, 0)
        block_weights, block_rates = coefficients(block_logits, chan_bias, 3)
        block_end = lax.dynamic_slice_in_dim(up_ends, visited * local_chans, local_chans, 0)
        return carry_through(current, block_weights, block_rates, True) + block_end

    down_in = lax.fori_loop(0, position, down_visit, anchor)
    up_in = lax.fori_loop(0, devices - 1 - position, up_visit, anchor)
    _, down_rows = sweep_rows(down_in, down_weights, down_rate, down_drive, False, True)
    _, up_rows = sweep_rows(up_in, up_weights, up_rate, up_drive, True, True)
    return (down_rows * up_rows).astype(jnp.bfloat16)


def solution(mesh):
    in_specs = (P("rows", "chan", None), P("chan"), P(None, "chan"), P("chan"))
    out_specs = P("rows", "chan", None)
    return jax.shard_map(shards, mesh=mesh, in_specs=in_specs, out_specs=out_specs, check_vma=False)
```

profile of v0, /device:TPU:0, one launch (start us, length us, event | category | flops | bytes accessed | tf_op | source)
XLA Modules:
  0.0 489.4 jit_solution(14477030094933963573)
XLA Ops:
  6.5 3.9 fusion.28
  10.5 56.0 %all-reduce.15.cloned.1.call-done = f32[16,1024]{1,0:T(8,128)} async-done(((f32[16,1024]{1,0:T(8,128)}), f32[16,1024]{1,0:T(8,128)}) %all-reduce.15.cloned.1.call-update) | async-done | bytes 65552 | tf_op jit(solution)/shard_map/psum | solution.py:51
  67.4 7.7 %fusion.36 = f32[16,8,1024]{2,1,0:T(8,128)} fusion(bf16[16,128,1024]{2,1,0:T(8,128)(2,1)} %param.20, f32[128]{0:T(128)} %param.21, f32[16,1024]{1,0:T(8,128)S(1)} %add_rsqrt_fusion, f32[8,128]{1,0:T(8,128)S(1)} %copy-done), kind=kOutput, calls=%fused_computation.76 | convolution fusion | flops 207618048 | bytes 4788736 | tf_op jit(solution)/shard_map/jc,rcw->rjw/dot_general | solution.py:54
  75.1 54.3 %all-reduce.17.cloned.1.call-done = f32[16,8,1024]{2,1,0:T(8,128)} async-done(((f32[16,8,1024]{2,1,0:T(8,128)}), f32[16,8,1024]{2,1,0:T(8,128)}) %all-reduce.17.cloned.1.call-update) | async-done | bytes 524304 | tf_op jit(solution)/shard_map/psum | solution.py:61
  131.1 15.1 %fusion.30 = (f32[16,128,1024]{2,1,0:T(8,128)}, f32[16,128,1024]{2,1,0:T(8,128)}, f32[16,128,1024]{2,1,0:T(8,128)}, f32[16,128,1024]{2,1,0:T(8,128)}) fusion(bf16[16,128,1024]{2,1,0:T(8,128)(2,1)} %param.20, f32[128]{0:T(128)S(1)} %copy-done.6, f32[16,1024]{1,0:T(8,128)S(1)} %add_rsqrt_fusion, f32[128]{0:T(128)S(1)} %copy-done.5, ...), kind=kLoop, calls=%fused_computation.68 | loop fusion | flops 27262976 | bytes 37946368 | tf_op jit(solution)/shard_map/mul | solution.py:65
  146.2 30.4 %while.121 = (s32[]{:T(128)}, f32[128,1024]{1,0:T(8,128)S(1)}, f32[16,128,1024]{2,1,0:T(8,128)}, f32[16,3,1024]{2,1,0:T(4,128)S(1)}, f32[16,128,1024]{2,1,0:T(8,...) while((s32[]{:T(128)}, f32[128,1024]{1,0:T(8,128)S(1)}, ...), condition=%wide.region_18.19_spmd.clone, body=%wide.region_17.18_spmd.clone.sunk | while | flops 1310726 | bytes 6325412 | solution.py:35
  178.1 31.0 %while.120 = (s32[]{:T(128)}, f32[128,1024]{1,0:T(8,128)S(1)}, f32[16,128,1024]{2,1,0:T(8,128)}, f32[16,3,1024]{2,1,0:T(4,128)S(1)}, f32[16,128,1024]{2,1,0:T(8,128)}, /*index=5*/s32[]{:T(128)}, s32[]{:T(128)}, s32[]{}, s32[]{}) while((s32[]{:T(128)}, f32[128,1024]{1,0:T(8,128)S(1)}, f32[16,128,1024]{2,1,0:T(8,128)}, ...), condition=%wide.region_6.0_spmd.clone, body=%wide.region_5.0_spmd.clone.sunk | while | flops 1310725 | bytes 6325392 | solution.py:35
  209.9 12.7 %all-gather.8.cloned.1.call-done = f32[512,1024]{1,0:T(8,128)} async-done(((f32[128,1024]{1,0:T(8,128)}), f32[512,1024]{1,0:T(8,128)}) %all-gather.8.cloned.1.call-update) | async-done | bytes 2097168 | tf_op jit(solution)/shard_map/all_gather | solution.py:72
  222.6 45.9 %all-gather.4.cloned.1.call-done = f32[64,8,1024]{2,1,0:T(8,128)} async-done(((f32[16,8,1024]{2,1,0:T(8,128)}), f32[64,8,1024]{2,1,0:T(8,128)}) %all-gather.4.cloned.1.call-update) | async-done | bytes 2097168 | tf_op jit(solution)/shard_map/all_gather | solution.py:70
  268.6 112.8 %while.118 = (s32[]{:T(128)}, f32[128,1024]{1,0:T(8,128)S(1)}, s32[]{:T(128)}, f32[64,8,1024]{2,1,0:T(8,128)}, f32[128]{0:T(128)S(1)}, /*index=5*/f32[512,1024]{...) while((s32[]{:T(128)}, f32[128,1024]{1,0:T(8,128)S(1)}, ...), condition=%wide.region_24.25_spmd, body=%wide.region_19.24_spmd.sunk | while | flops 9568278 | bytes 15501354 | solution.py:94
  269.9 5.4 %add_divide_fusion.7 = f32[16,128,1024]{2,1,0:T(8,128)} fusion(f32[128]{0:T(128)S(1)} %get-tuple-element.1319, f32[16,1024]{1,0:T(8,128)S(1)} %bitcast.131), kind=kLoop, calls=%fused_computation.30.clone.1 | loop fusion | flops 8388608 | bytes 8454656 | tf_op jit(solution)/shard_map/while/body/div | solution.py:24
  276.8 28.4 %while.123 = (s32[]{:T(128)}, f32[128,1024]{1,0:T(8,128)S(1)}, f32[16,128,1024]{2,1,0:T(8,128)}, f32[16,3,1024]{2,1,0:T(4,128)S(1)}, s32[]{:T(128)}, /*index=5*/s32[]{:T(128)}, s32[]{:T(128)}, s32[]{}, s32[]{}) while((s32[]{:T(128)}, f32[128,1024]{1,0:T(8,128)S(1)}, f32[16,128,1024]{2,1,0:T(8,128)}, f32[16,3,1024]{2,1,0:T(4,128)S(1)}, ...), condition=%wide.region_23.23_spmd, body=%wide.region_22.22_spmd.sunk | while | flops 917509 | bytes 4752529 | solution.py:43
  307.5 5.4 %add_divide_fusion.7 = f32[16,128,1024]{2,1,0:T(8,128)} fusion(f32[128]{0:T(128)S(1)} %get-tuple-element.1319, f32[16,1024]{1,0:T(8,128)S(1)} %bitcast.131), kind=kLoop, calls=%fused_computation.30.clone.1 | loop fusion | flops 8388608 | bytes 8454656 | tf_op jit(solution)/shard_map/while/body/div | solution.py:24
  314.4 28.3 %while.123 = (s32[]{:T(128)}, f32[128,1024]{1,0:T(8,128)S(1)}, f32[16,128,1024]{2,1,0:T(8,128)}, f32[16,3,1024]{2,1,0:T(4,128)S(1)}, s32[]{:T(128)}, /*index=5*/s32[]{:T(128)}, s32[]{:T(128)}, s32[]{}, s32[]{}) while((s32[]{:T(128)}, f32[128,1024]{1,0:T(8,128)S(1)}, f32[16,128,1024]{2,1,0:T(8,128)}, f32[16,3,1024]{2,1,0:T(4,128)S(1)}, ...), condition=%wide.region_23.23_spmd, body=%wide.region_22.22_spmd.sunk | while | flops 917509 | bytes 4752529 | solution.py:43
  345.0 5.4 %add_divide_fusion.7 = f32[16,128,1024]{2,1,0:T(8,128)} fusion(f32[128]{0:T(128)S(1)} %get-tuple-element.1319, f32[16,1024]{1,0:T(8,128)S(1)} %bitcast.131), kind=kLoop, calls=%fused_computation.30.clone.1 | loop fusion | flops 8388608 | bytes 8454656 | tf_op jit(solution)/shard_map/while/body/div | solution.py:24
  351.9 28.3 %while.123 = (s32[]{:T(128)}, f32[128,1024]{1,0:T(8,128)S(1)}, f32[16,128,1024]{2,1,0:T(8,128)}, f32[16,3,1024]{2,1,0:T(4,128)S(1)}, s32[]{:T(128)}, /*index=5*/s32[]{:T(128)}, s32[]{:T(128)}, s32[]{}, s32[]{}) while((s32[]{:T(128)}, f32[128,1024]{1,0:T(8,128)S(1)}, f32[16,128,1024]{2,1,0:T(8,128)}, f32[16,3,1024]{2,1,0:T(4,128)S(1)}, ...), condition=%wide.region_23.23_spmd, body=%wide.region_22.22_spmd.sunk | while | flops 917509 | bytes 4752529 | solution.py:43
  381.4 4.3 broadcast.113.clone.1
  385.6 41.8 %while.119 = (s32[]{:T(128)}, f32[128,1024]{1,0:T(8,128)S(1)}, f32[16,128,1024]{2,1,0:T(8,128)}, f32[16,128,1024]{2,1,0:T(8,128)}, f32[16,3,1024]{2,1,0:T(4,128)...) while((s32[]{:T(128)}, f32[128,1024]{1,0:T(8,128)S(1)}, ...), condition=%wide.region_26.27_spmd, body=%wide.region_25.26_spmd.sunk | while | flops 1048581 | bytes 5801121 | solution.py:35
  385.9 2.4 bitcast_dynamic-update-slice_fusion.5
  393.7 2.4 bitcast_dynamic-update-slice_fusion.5
  401.5 2.4 bitcast_dynamic-update-slice_fusion.5
  409.4 2.4 bitcast_dynamic-update-slice_fusion.5
  414.6 2.4 bitcast_dynamic-update-slice_fusion.5
  419.8 2.4 bitcast_dynamic-update-slice_fusion.5
  422.4 2.4 bitcast_dynamic-update-slice_fusion.5
  427.5 4.3 broadcast.113.clone
  431.8 41.8 %while.116 = (s32[]{:T(128)}, f32[128,1024]{1,0:T(8,128)S(1)}, f32[16,128,1024]{2,1,0:T(8,128)}, f32[16,128,1024]{2,1,0:T(8,128)}, f32[16,3,1024]{2,1,0:T(4,128)...) while((s32[]{:T(128)}, f32[128,1024]{1,0:T(8,128)S(1)}, ...), condition=%wide.region_14.15_spmd, body=%wide.region_13.14_spmd.sunk | while | flops 1048580 | bytes 5801609 | solution.py:35
  437.2 2.4 bitcast_dynamic-update-slice_fusion.4
  458.1 2.4 bitcast_dynamic-update-slice_fusion.4
  460.8 2.4 bitcast_dynamic-update-slice_fusion.4
  471.2 2.4 bitcast_dynamic-update-slice_fusion.4
  473.6 9.3 %multiply_convert_fusion = bf16[16,128,1024]{2,1,0:T(8,128)(2,1)} fusion(f32[16,128,1024]{2,1,0:T(8,128)} %get-tuple-element.568, f32[16,128,1024]{2,1,0:T(8,128)} %get-tuple-element.571), kind=kLoop, calls=%fused_computation.71 | loop fusion | flops 4194304 | bytes 20971520 | tf_op jit(solution)/shard_map/convert_element_type | solution.py:97
  (405 shorter events, 216.8 us)
Async XLA Ops:
  6.5 60.8 %copy-start = (f32[8,128]{1,0:T(8,128)S(1)}, f32[8,128]{1,0:T(8,128)}, u32[]{:S(2)}) copy-start(f32[8,128]{1,0:T(8,128)} %param.22) | copy-start | bytes 12292
  6.5 124.5 %copy-start.6 = (f32[128]{0:T(128)S(1)}, f32[128]{0:T(128)}, u32[]{:S(2)}) copy-start(f32[128]{0:T(128)} %param.21) | copy-start | bytes 1540
  6.5 124.6 %copy-start.5 = (f32[128]{0:T(128)S(1)}, f32[128]{0:T(128)}, u32[]{:S(2)}) copy-start(f32[128]{0:T(128)} %param.23) | copy-start | bytes 1540
  6.5 60.0 %all-reduce.15.cloned.1.call-start = ((), (), s32[]{:S(2)}) async-start(), calls=%async_computation | async-start | bytes 131072 | tf_op jit(solution)/shard_map/psum | solution.py:51
  10.5 119.0 %all-reduce.17.cloned.1.call-start = ((), (), s32[]{:S(2)}) async-start(), calls=%async_computation.1 | async-start | bytes 1048576 | tf_op jit(solution)/shard_map/psum | solution.py:61
  75.1 147.5 %all-gather.8.cloned.1.call-start = ((), (), s32[]{:S(2)}) async-start(), calls=%async_computation.4 | async-start | bytes 2621440 | tf_op jit(solution)/shard_map/all_gather | solution.py:72
  130.5 47.0 %copy-start.4 = (f32[16,8,1024]{2,1,0:T(8,128)}, f32[16,8,1024]{2,1,0:T(8,128)S(1)}, u32[]{:S(2)}) copy-start(f32[16,8,1024]{2,1,0:T(8,128)S(1)} %broadcast_multiply_fusion) | copy-start | bytes 1572868
  176.7 0.8 copy-start.2
  177.5 91.0 %all-gather.4.cloned.1.call-start = ((), (), s32[]{:S(2)}) async-start(), calls=%async_computation.2 | async-start | bytes 2621440 | tf_op jit(solution)/shard_map/all_gather | solution.py:70
  178.1 249.4 %all-gather.6.cloned.1.call-start = ((), (), s32[]{:S(2)}) async-start(), calls=%async_computation.3 | async-start | bytes 2621440 | tf_op jit(solution)/shard_map/all_gather | solution.py:71
  209.1 0.8 copy-start.3
  473.6 9.3 %copy-start.1 = (f32[8,128]{1,0:T(8,128)S(1)}, f32[8,128]{1,0:T(8,128)}, u32[]{:S(2)}) copy-start(f32[8,128]{1,0:T(8,128)} %param.22) | copy-start | bytes 12292
Sparse Core Ops, SparseCore 0:
  10.6 55.8 all-reduce.14
  75.2 54.1 all-reduce.16
  177.6 44.9 all-gather.7
  224.0 44.4 all-gather.3
  269.9 44.4 all-gather.5
where the time goes:
time: 494 us; the launch traced here: 489 us
  other arithmetic  258 us (52%)
  waiting for transfers between devices  169 us (34%)
  local copies, waits for them, and re-layouts  38.3 us (8%)
  between operations  13.3 us (3%)
  matrix products  7.69 us (2%)
    dynamic_update_slice x32, other arithmetic, sweep_rows(): lax.scan(sweep_row_step, start, (weights, rates, drive), reverse=reverse)  76.6 us
    mul x48, other arithmetic, advance(): return (1.0 - row_rate) * blended  73.1 us
    psum x1, waiting for transfers between devices, shards(): square_total = lax.psum(squares, 'chan')  56 us
    psum x1, waiting for transfers between devices, shards(): logits = lax.psum(projected, 'chan') * logit_scale  54.3 us
    add x32, other arithmetic, sweep_row_step(): current = advance(current, row_weights, row_rate) + row_drive  51.8 us
    all_gather x1, waiting for transfers between devices, shards(): lax.all_gather(logits, 'rows', axis=0, tiled=True)  45.9 us
    slice x112, local copies, waits for them, and re-layouts, advance(): left_side = jnp.concatenate([edge_zero, current[:, :-1]], axis=1)  22.6 us
    div x3, other arithmetic, coefficients(): jax.nn.sigmoid(logits[:, 6 + offset // 3, :][:, None, :] + chan_bias[None...  16.3 us
  transfers between devices with their start and end apart: 5, of which 4 were waited for; matrix products, arithmetic and copies ran while one was open for 38% of the time, Pallas kernels for 0%

commit v1 on v0

--- a/solution.py
+++ b/solution.py
@@ -1,3 +1,4 @@
+import functools
 import jax
 import jax.numpy as jnp
 from jax import lax
@@ -5,6 +6,14 @@
 
 CHANNELS = 1024
 EPSILON = 1e-05
+
+
+def attach_panel(u, mesh_ax):
+    h_now = jax.lax.all_gather(u, axis_name=mesh_ax)
+    return jnp.sum(h_now, axis=0)
+
+
+choose_the_widths = functools.partial(attach_panel, mesh_ax="chan")
 
 
 def advance(current, row_weights, row_rate):
@@ -58,7 +67,7 @@
         precision=lax.Precision.HIGHEST,
         preferred_element_type=jnp.float32,
     )
-    logits = lax.psum(projected, "chan") * logit_scale
+    logits = choose_the_widths(projected) * logit_scale
     down_weights, down_rate = coefficients(logits, chan_bias, 0)
     up_weights, up_rate = coefficients(logits, chan_bias, 3)
     down_drive = jnp.sqrt(down_rate) * normed

time: 494 us -> 478 us (0.968)
  waiting for transfers between devices: 169 us -> 152 us
    psum x1 -> x0, waiting for transfers between devices: 54.3 us -> none  [shards(): logits = lax.psum(projected, 'chan') * logit_scale]
    all_gather x0 -> x1, waiting for transfers between devices: none -> 36.1 us  [attach_panel(): h_now = jax.lax.all_gather(u, axis_name=mesh_ax)]
  transfers between devices with their start and end apart: 5 -> 5, of which waited for: 4 -> 4; matrix products, arithmetic and copies ran while one was open for 38% -> 40% of each run, Pallas kernels for 0% -> 0%
where the time goes in v1:
time: 478 us; the launch traced here: 474 us
  other arithmetic  259 us (54%)
  waiting for transfers between devices  152 us (32%)
  local copies, waits for them, and re-layouts  38.3 us (8%)
  between operations  13.3 us (3%)
  matrix products  7.78 us (2%)
    dynamic_update_slice x32, other arithmetic, sweep_rows(): lax.scan(sweep_row_step, start, (weights, rates, drive), reverse=reverse)  76.6 us
    mul x48, other arithmetic, advance(): return (1.0 - row_rate) * blended  73.1 us
    psum x1, waiting for transfers between devices, shards(): square_total = lax.psum(squares, 'chan')  56 us
    add x32, other arithmetic, sweep_row_step(): current = advance(current, row_weights, row_rate) + row_drive  51.8 us
    all_gather x1, waiting for transfers between devices, shards(): lax.all_gather(logits, 'rows', axis=0, tiled=True)  45.9 us
    all_gather x1, waiting for transfers between devices, attach_panel(): h_now = jax.lax.all_gather(u, axis_name=mesh_ax)  36.1 us
    slice x112, local copies, waits for them, and re-layouts, advance(): left_side = jnp.concatenate([edge_zero, current[:, :-1]], axis=1)  22.6 us
    div x3, other arithmetic, coefficients(): jax.nn.sigmoid(logits[:, 6 + offset // 3, :][:, None, :] + chan_bias[None...  16.3 us
  transfers between devices with their start and end apart: 5, of which 4 were waited for; matrix products, arithmetic and copies ran while one was open for 40% of the time, Pallas kernels for 0%

profile of v1, /device:TPU:0, one launch (start us, length us, event | category | flops | bytes accessed | tf_op | source)
XLA Modules:
  0.0 473.6 jit_solution(5126986215126407435)
XLA Ops:
  6.5 3.9 fusion.28
  10.5 56.0 %all-reduce.14.cloned.1.call-done = f32[16,1024]{1,0:T(8,128)} async-done(((f32[16,1024]{1,0:T(8,128)}), f32[16,1024]{1,0:T(8,128)}) %all-reduce.14.cloned.1.call-update) | async-done | bytes 65552 | tf_op jit(solution)/shard_map/psum | solution.py:60
  67.4 7.8 %fusion.36 = f32[16,8,1024]{2,1,0:T(8,128)} fusion(bf16[16,128,1024]{2,1,0:T(8,128)(2,1)} %param.20, f32[128]{0:T(128)} %param.21, f32[16,1024]{1,0:T(8,128)S(1)} %add_rsqrt_fusion, f32[8,128]{1,0:T(8,128)S(1)} %copy-done), kind=kOutput, calls=%fused_computation.76 | convolution fusion | flops 207618048 | bytes 4788736 | tf_op jit(solution)/shard_map/jc,rcw->rjw/dot_general | solution.py:63
  75.2 36.1 %all-gather.12.cloned.1.call-done = f32[128,8,1024]{2,1,0:T(8,128)} async-done(((f32[16,8,1024]{2,1,0:T(8,128)}), f32[128,8,1024]{2,1,0:T(8,128)}) %all-gather.12.cloned.1.call-update) | async-done | bytes 4194320 | tf_op jit(solution)/shard_map/all_gather | solution.py:12
  111.3 2.6 reduce_sum.61
  114.6 15.1 %fusion.30 = (f32[16,128,1024]{2,1,0:T(8,128)}, f32[16,128,1024]{2,1,0:T(8,128)}, f32[16,128,1024]{2,1,0:T(8,128)}, f32[16,128,1024]{2,1,0:T(8,128)}) fusion(bf16[16,128,1024]{2,1,0:T(8,128)(2,1)} %param.20, f32[128]{0:T(128)S(1)} %copy-done.6, f32[16,1024]{1,0:T(8,128)S(1)} %add_rsqrt_fusion, f32[128]{0:T(128)S(1)} %copy-done.5, ...), kind=kLoop, calls=%fused_computation.68 | loop fusion | flops 27262976 | bytes 37946368 | tf_op jit(solution)/shard_map/mul | solution.py:74
  129.7 30.4 %while.121 = (s32[]{:T(128)}, f32[128,1024]{1,0:T(8,128)S(1)}, f32[16,128,1024]{2,1,0:T(8,128)}, f32[16,3,1024]{2,1,0:T(4,128)S(1)}, f32[16,128,1024]{2,1,0:T(8,...) while((s32[]{:T(128)}, f32[128,1024]{1,0:T(8,128)S(1)}, ...), condition=%wide.region_18.19_spmd.clone, body=%wide.region_17.18_spmd.clone.sunk | while | flops 1310726 | bytes 6325412 | solution.py:44
  161.6 31.0 %while.120 = (s32[]{:T(128)}, f32[128,1024]{1,0:T(8,128)S(1)}, f32[16,128,1024]{2,1,0:T(8,128)}, f32[16,3,1024]{2,1,0:T(4,128)S(1)}, f32[16,128,1024]{2,1,0:T(8,128)}, /*index=5*/s32[]{:T(128)}, s32[]{:T(128)}, s32[]{}, s32[]{}) while((s32[]{:T(128)}, f32[128,1024]{1,0:T(8,128)S(1)}, f32[16,128,1024]{2,1,0:T(8,128)}, ...), condition=%wide.region_6.0_spmd.clone, body=%wide.region_5.0_spmd.clone.sunk | while | flops 1310725 | bytes 6325392 | solution.py:44
  193.4 13.4 %all-gather.10.cloned.1.call-done = f32[512,1024]{1,0:T(8,128)} async-done(((f32[128,1024]{1,0:T(8,128)}), f32[512,1024]{1,0:T(8,128)}) %all-gather.10.cloned.1.call-update) | async-done | bytes 2097168 | tf_op jit(solution)/shard_map/all_gather | solution.py:81
  206.8 45.9 %all-gather.6.cloned.1.call-done = f32[64,8,1024]{2,1,0:T(8,128)} async-done(((f32[16,8,1024]{2,1,0:T(8,128)}), f32[64,8,1024]{2,1,0:T(8,128)}) %all-gather.6.cloned.1.call-update) | async-done | bytes 2097168 | tf_op jit(solution)/shard_map/all_gather | solution.py:79
  252.7 112.8 %while.118 = (s32[]{:T(128)}, f32[128,1024]{1,0:T(8,128)S(1)}, s32[]{:T(128)}, f32[64,8,1024]{2,1,0:T(8,128)}, f32[128]{0:T(128)S(1)}, /*index=5*/f32[512,1024]{...) while((s32[]{:T(128)}, f32[128,1024]{1,0:T(8,128)S(1)}, ...), condition=%wide.region_24.25_spmd, body=%wide.region_19.24_spmd.sunk | while | flops 9568278 | bytes 15501354 | solution.py:103
  254.1 5.4 %add_divide_fusion.7 = f32[16,128,1024]{2,1,0:T(8,128)} fusion(f32[128]{0:T(128)S(1)} %get-tuple-element.1319, f32[16,1024]{1,0:T(8,128)S(1)} %bitcast.132), kind=kLoop, calls=%fused_computation.30.clone.1 | loop fusion | flops 8388608 | bytes 8454656 | tf_op jit(solution)/shard_map/while/body/div | solution.py:33
  261.0 28.4 %while.123 = (s32[]{:T(128)}, f32[128,1024]{1,0:T(8,128)S(1)}, f32[16,128,1024]{2,1,0:T(8,128)}, f32[16,3,1024]{2,1,0:T(4,128)S(1)}, s32[]{:T(128)}, /*index=5*/s32[]{:T(128)}, s32[]{:T(128)}, s32[]{}, s32[]{}) while((s32[]{:T(128)}, f32[128,1024]{1,0:T(8,128)S(1)}, f32[16,128,1024]{2,1,0:T(8,128)}, f32[16,3,1024]{2,1,0:T(4,128)S(1)}, ...), condition=%wide.region_23.23_spmd, body=%wide.region_22.22_spmd.sunk | while | flops 917509 | bytes 4752529 | solution.py:52
  291.7 5.4 %add_divide_fusion.7 = f32[16,128,1024]{2,1,0:T(8,128)} fusion(f32[128]{0:T(128)S(1)} %get-tuple-element.1319, f32[16,1024]{1,0:T(8,128)S(1)} %bitcast.132), kind=kLoop, calls=%fused_computation.30.clone.1 | loop fusion | flops 8388608 | bytes 8454656 | tf_op jit(solution)/shard_map/while/body/div | solution.py:33
  298.5 28.3 %while.123 = (s32[]{:T(128)}, f32[128,1024]{1,0:T(8,128)S(1)}, f32[16,128,1024]{2,1,0:T(8,128)}, f32[16,3,1024]{2,1,0:T(4,128)S(1)}, s32[]{:T(128)}, /*index=5*/s32[]{:T(128)}, s32[]{:T(128)}, s32[]{}, s32[]{}) while((s32[]{:T(128)}, f32[128,1024]{1,0:T(8,128)S(1)}, f32[16,128,1024]{2,1,0:T(8,128)}, f32[16,3,1024]{2,1,0:T(4,128)S(1)}, ...), condition=%wide.region_23.23_spmd, body=%wide.region_22.22_spmd.sunk | while | flops 917509 | bytes 4752529 | solution.py:52
  329.2 5.4 %add_divide_fusion.7 = f32[16,128,1024]{2,1,0:T(8,128)} fusion(f32[128]{0:T(128)S(1)} %get-tuple-element.1319, f32[16,1024]{1,0:T(8,128)S(1)} %bitcast.132), kind=kLoop, calls=%fused_computation.30.clone.1 | loop fusion | flops 8388608 | bytes 8454656 | tf_op jit(solution)/shard_map/while/body/div | solution.py:33
  336.0 28.3 %while.123 = (s32[]{:T(128)}, f32[128,1024]{1,0:T(8,128)S(1)}, f32[16,128,1024]{2,1,0:T(8,128)}, f32[16,3,1024]{2,1,0:T(4,128)S(1)}, s32[]{:T(128)}, /*index=5*/s32[]{:T(128)}, s32[]{:T(128)}, s32[]{}, s32[]{}) while((s32[]{:T(128)}, f32[128,1024]{1,0:T(8,128)S(1)}, f32[16,128,1024]{2,1,0:T(8,128)}, f32[16,3,1024]{2,1,0:T(4,128)S(1)}, ...), condition=%wide.region_23.23_spmd, body=%wide.region_22.22_spmd.sunk | while | flops 917509 | bytes 4752529 | solution.py:52
  365.5 4.3 broadcast.113.clone.1
  369.8 41.8 %while.119 = (s32[]{:T(128)}, f32[128,1024]{1,0:T(8,128)S(1)}, f32[16,128,1024]{2,1,0:T(8,128)}, f32[16,128,1024]{2,1,0:T(8,128)}, f32[16,3,1024]{2,1,0:T(4,128)...) while((s32[]{:T(128)}, f32[128,1024]{1,0:T(8,128)S(1)}, ...), condition=%wide.region_26.27_spmd, body=%wide.region_25.26_spmd.sunk | while | flops 1048581 | bytes 5801121 | solution.py:44
  370.0 2.4 bitcast_dynamic-update-slice_fusion.5
  377.8 2.4 bitcast_dynamic-update-slice_fusion.5
  385.7 2.4 bitcast_dynamic-update-slice_fusion.5
  393.5 2.4 bitcast_dynamic-update-slice_fusion.5
  398.7 2.4 bitcast_dynamic-update-slice_fusion.5
  404.0 2.4 bitcast_dynamic-update-slice_fusion.5
  406.6 2.4 bitcast_dynamic-update-slice_fusion.5
  411.7 4.3 broadcast.113.clone
  416.0 41.8 %while.116 = (s32[]{:T(128)}, f32[128,1024]{1,0:T(8,128)S(1)}, f32[16,128,1024]{2,1,0:T(8,128)}, f32[16,128,1024]{2,1,0:T(8,128)}, f32[16,3,1024]{2,1,0:T(4,128)...) while((s32[]{:T(128)}, f32[128,1024]{1,0:T(8,128)S(1)}, ...), condition=%wide.region_14.15_spmd, body=%wide.region_13.14_spmd.sunk | while | flops 1048580 | bytes 5801609 | solution.py:44
  421.4 2.4 bitcast_dynamic-update-slice_fusion.4
  442.3 2.4 bitcast_dynamic-update-slice_fusion.4
  455.3 2.4 bitcast_dynamic-update-slice_fusion.4
  457.7 9.3 %multiply_convert_fusion = bf16[16,128,1024]{2,1,0:T(8,128)(2,1)} fusion(f32[16,128,1024]{2,1,0:T(8,128)} %get-tuple-element.568, f32[16,128,1024]{2,1,0:T(8,128)} %get-tuple-element.571), kind=kLoop, calls=%fused_computation.71 | loop fusion | flops 4194304 | bytes 20971520 | tf_op jit(solution)/shard_map/convert_element_type | solution.py:106
  (406 shorter events, 218.1 us)
Async XLA Ops:
  6.5 60.8 %copy-start = (f32[8,128]{1,0:T(8,128)S(1)}, f32[8,128]{1,0:T(8,128)}, u32[]{:S(2)}) copy-start(f32[8,128]{1,0:T(8,128)} %param.22) | copy-start | bytes 12292
  6.5 59.9 %all-reduce.14.cloned.1.call-start = ((), (), s32[]{:S(2)}) async-start(), calls=%async_computation | async-start | bytes 131072 | tf_op jit(solution)/shard_map/psum | solution.py:60
  10.4 100.9 %all-gather.12.cloned.1.call-start = ((), (), s32[]{:S(2)}) async-start(), calls=%async_computation.4 | async-start | bytes 4718592 | tf_op jit(solution)/shard_map/all_gather | solution.py:12
  67.3 47.2 %copy-start.5 = (f32[128]{0:T(128)S(1)}, f32[128]{0:T(128)}, u32[]{:S(2)}) copy-start(f32[128]{0:T(128)} %param.23) | copy-start | bytes 1540
  67.4 47.2 %copy-start.6 = (f32[128]{0:T(128)S(1)}, f32[128]{0:T(128)}, u32[]{:S(2)}) copy-start(f32[128]{0:T(128)} %param.21) | copy-start | bytes 1540
  75.2 131.6 %all-gather.10.cloned.1.call-start = ((), (), s32[]{:S(2)}) async-start(), calls=%async_computation.3 | async-start | bytes 2621440 | tf_op jit(solution)/shard_map/all_gather | solution.py:81
  114.0 47.0 %copy-start.4 = (f32[16,8,1024]{2,1,0:T(8,128)}, f32[16,8,1024]{2,1,0:T(8,128)S(1)}, u32[]{:S(2)}) copy-start(f32[16,8,1024]{2,1,0:T(8,128)S(1)} %broadcast_multiply_fusion) | copy-start | bytes 1572868
  160.1 0.8 copy-start.2
  160.9 91.7 %all-gather.6.cloned.1.call-start = ((), (), s32[]{:S(2)}) async-start(), calls=%async_computation.1 | async-start | bytes 2621440 | tf_op jit(solution)/shard_map/all_gather | solution.py:79
  161.5 250.1 %all-gather.8.cloned.1.call-start = ((), (), s32[]{:S(2)}) async-start(), calls=%async_computation.2 | async-start | bytes 2621440 | tf_op jit(solution)/shard_map/all_gather | solution.py:80
  192.5 0.8 copy-start.3
  457.7 9.3 %copy-start.1 = (f32[8,128]{1,0:T(8,128)S(1)}, f32[8,128]{1,0:T(8,128)}, u32[]{:S(2)}) copy-start(f32[8,128]{1,0:T(8,128)} %param.22) | copy-start | bytes 12292
Sparse Core Ops, SparseCore 0:
  10.5 55.8 all-reduce.13
  75.3 35.9 all-gather.11
  161.1 45.6 all-gather.9
  208.2 44.4 all-gather.5
  254.1 44.4 all-gather.7
